TPU v7x, 256 devices: a whole 4x4x8 slice. The times are simulated.
256 devices in a mesh: seq: 16 (over y, z_hi, core), mp: 16 (over z_lo, x).
Axes of the slice: x: 4, y: 4, z: 8 (z_hi: 2, z_lo: 4; z = z_hi * 4 + z_lo), core: 2. Of those that a mesh axis runs over, the one named last changes fastest.
Arguments:
- hidden_in: bfloat16 [2048, 2048], P('seq'), may hold values from -0.59765625 to 0.59765625
- input_gain: float32 [2048], replicated, may hold values from 0.25 to 1.75
- w_query: bfloat16 [2048, 2048], P(None, 'mp'), may hold values from -0.125 to 0.125
- key_value_weight: bfloat16 [2048, 4096], P(None, 'mp'), may hold values from -1 to 1, as said below
- query_gain: float32 [128], replicated, may hold values from 0.25 to 1.75
- key_gain: float32 [128], replicated, may hold values from 0.25 to 1.75
- w_out: bfloat16 [2048, 2048], P('mp'), may hold values from -0.125 to 0.125
- post_gain: float32 [2048], replicated, may hold values from 0.25 to 1.75
- w_gate: bfloat16 [2048, 6144], P(None, 'mp'), may hold values from -0.125 to 0.125
- w_up: bfloat16 [2048, 6144], P(None, 'mp'), may hold values from -0.125 to 0.125
- w_down: bfloat16 [6144, 2048], P('mp'), may hold values from -0.078125 to 0.078125
- prefix_slot_cache: bfloat16 [32, 256, 8, 256], P('seq'), may hold values from -240 to 240, as said below
- block_table: int32 [32], replicated, may hold values from 0 to 31, each once
- request_prefix: int32 [32], replicated, may hold values from 0 to 3
- suffix_lengths: int32 [32], replicated, may hold values from 1 to 256, 2048 in all
Outputs:
- hidden_out: bfloat16 [2048, 2048], P('seq', 'mp')
- suffix_key_values: bfloat16 [2048, 2048], P('seq', 'mp')
Inputs may be any that keep to these rules, and one draw needn't show every extreme that they name: block_table[p * 8 + i] is the slot holding block i of prefix p; every slot appears once. `suffix_lengths`: the lengths add up to 2048 and the longest is exactly 256. `prefix_slot_cache`: per slot, position and key-value head: a key in the first 128 entries, a value in the last 128. `key_value_weight`: columns of key-value head k: 2 equal blocks of 256, starting at k * 2 * 2 * 128.
All inputs are finite; a program needn't handle non-finite values.
Results may differ from a plain program's by a relative error of at most 0.025.
The roundings to bfloat16 on the way count: a program that leaves them out, or rounds other values in their place, can miss the bound.
Values may be sent and summed in bfloat16 or wider, within the bound.
A program may use at most 64 MiB of HBM per device.

v0:
```python
import math
import jax
import jax.numpy as jnp
from jax import lax
from jax.sharding import PartitionSpec as P

QUERY_HEADS = 16
KEY_VALUE_HEADS = 8
HEAD_WIDTH = 128
N_PREFIX = 4
EPSILON = 1e-06
THETA = 1000000.0
NEGATIVE_FLOOR = -1e30


def token_tables(request_prefix, suffix_lengths, positions, prefix_length):
    request_ends = jnp.cumsum(suffix_lengths)
    starts = request_ends - suffix_lengths
    inside = (
        (positions[:, None] >= starts[None, :]) & (positions[:, None] < request_ends[None, :])
    ).astype(jnp.int32)
    request_ids = jnp.arange(suffix_lengths.shape[0], dtype=jnp.int32)
    request_of = jnp.sum(inside * request_ids[None, :], axis=1)
    start_of = jnp.sum(inside * starts[None, :], axis=1)
    prefix_of = jnp.sum(inside * request_prefix[None, :], axis=1)
    rotary_pos = prefix_length + positions - start_of
    return (request_of, prefix_of, rotary_pos)


def row_norm(values, gain):
    return values * lax.rsqrt(jnp.mean(values * values, axis=-1, keepdims=True) + EPSILON) * gain


def head_norm(values, gain):
    return values * lax.rsqrt(jnp.mean(values * values, axis=-1, keepdims=True) + EPSILON) * gain


def rotate(values, rotary_pos):
    half_dim = values.shape[-1] // 2
    freq_ids = jnp.arange(half_dim).astype(jnp.float32)
    inverse = jnp.exp(freq_ids * (-2.0 * math.log(THETA) / values.shape[-1]))
    angles = rotary_pos.astype(jnp.float32)[:, None] * inverse[None, :]
    cosine = jnp.cos(angles)[:, None, :]
    sine_part = jnp.sin(angles)[:, None, :]
    first_half = values[..., :half_dim]
    second_half = values[..., half_dim:]
    return jnp.concatenate(
        [
            first_half * cosine - second_half * sine_part,
            second_half * cosine + first_half * sine_part,
        ],
        axis=-1,
    )


def allowed_keys(query_req, query_pre, query_pos, key_pre, key_req, key_pos):
    same_prefix = key_pre[None, :] == query_pre[:, None]
    same_request = (key_req[None, :] == query_req[:, None]) & (
        key_pos[None, :] <= query_pos[:, None]
    )
    return same_prefix | same_request


def group_partial(query_rows_all, allowed, key_row_block, value_row_block):
    scaling = 1.0 / math.sqrt(query_rows_all.shape[-1])
    scores = (
        jnp.einsum(
            "nkgd,mkd->nkgm", query_rows_all, key_row_block, preferred_element_type=jnp.float32
        )
        * scaling
    )
    allowed_full = allowed[:, None, None, :]
    scores = jnp.where(allowed_full, scores, NEGATIVE_FLOOR)
    highest_score = jnp.max(scores, axis=-1)
    weights = jnp.where(allowed_full, jnp.exp(scores - highest_score[..., None]), 0.0)
    total_weight = jnp.sum(weights, axis=-1)
    rounded = weights.astype(jnp.bfloat16)
    summed = jnp.einsum(
        "nkgm,mkd->nkgd", rounded, value_row_block, preferred_element_type=jnp.float32
    )
    layer_output = (summed / jnp.maximum(total_weight, 1.0)[..., None]).astype(jnp.bfloat16)
    return (highest_score, total_weight, layer_output)


def tile_partials(query_rows, query_req, query_pre, query_pos, bundle, tile_rows):
    key_row_block, value_row_block, key_pre, key_req, key_pos = bundle
    token_count = query_rows.shape[0]
    tile_count = token_count // tile_rows
    shaped = (
        query_rows.reshape((tile_count, tile_rows) + query_rows.shape[1:]),
        query_req.reshape(tile_count, tile_rows),
        query_pre.reshape(tile_count, tile_rows),
        query_pos.reshape(tile_count, tile_rows),
    )

    def one_tile(members):
        tile_queries, tile_req, tile_pre, tile_pos = members
        allowed = allowed_keys(tile_req, tile_pre, tile_pos, key_pre, key_req, key_pos)

        def computed(unused):
            return group_partial(tile_queries, allowed, key_row_block, value_row_block)

        def skipped(unused):
            stats_shape = tile_queries.shape[:-1]
            return (
                jnp.full(stats_shape, NEGATIVE_FLOOR, jnp.float32),
                jnp.zeros(stats_shape, jnp.float32),
                jnp.zeros(tile_queries.shape, jnp.bfloat16),
            )

        return lax.cond(jnp.any(allowed), computed, skipped, 0)

    highest_score, total_weight, layer_output = lax.map(one_tile, shaped)
    stats_shape = (token_count,) + query_rows.shape[1:-1]
    return (
        highest_score.reshape(stats_shape),
        total_weight.reshape(stats_shape),
        layer_output.reshape(query_rows.shape),
    )


def local(
    hidden_in,
    input_gain,
    w_query,
    key_value_weight,
    query_gain,
    key_gain,
    w_out,
    post_gain,
    w_gate,
    w_up,
    w_down,
    prefix_slot_cache,
    block_table,
    request_prefix,
    suffix_lengths,
):
    seq_count = lax.axis_size("seq")
    model_count = lax.axis_size("mp")
    my_seq = lax.axis_index("seq")
    my_model = lax.axis_index("mp")
    rows_here = hidden_in.shape[0]
    local_heads = w_query.shape[1] // HEAD_WIDTH
    group_width = QUERY_HEADS // KEY_VALUE_HEADS
    shared_heads = max(1, local_heads // group_width)
    query_per_head = local_heads // shared_heads
    pair_width = 2 * HEAD_WIDTH
    first_shared = my_model * local_heads // group_width
    blocks_here = prefix_slot_cache.shape[0]
    block_rows = prefix_slot_cache.shape[1]
    cache_extent = blocks_here * block_rows
    slot_total = blocks_here * seq_count
    prefix_length = slot_total // N_PREFIX * block_rows
    all_tokens = rows_here * seq_count
    hidden_f32 = hidden_in.astype(jnp.float32)
    normed = row_norm(hidden_f32, input_gain).astype(jnp.bfloat16)
    own_pos = my_seq * rows_here + jnp.arange(rows_here, dtype=jnp.int32)
    own_req, own_pre, own_rot = token_tables(request_prefix, suffix_lengths, own_pos, prefix_length)
    query_raw = jnp.dot(normed, w_query, preferred_element_type=jnp.float32).reshape(
        rows_here, local_heads, HEAD_WIDTH
    )
    query_rows_all = rotate(head_norm(query_raw, query_gain), own_rot).astype(jnp.bfloat16)
    pair_block = jnp.dot(normed, key_value_weight, preferred_element_type=jnp.float32).astype(
        jnp.bfloat16
    )
    share_ratio = max(1, group_width // local_heads)
    pair_split = pair_block.reshape(rows_here, shared_heads, 2, HEAD_WIDTH)
    key_row_block = rotate(
        head_norm(pair_split[:, :, 0].astype(jnp.float32), key_gain), own_rot
    ).astype(jnp.bfloat16)
    pairs_mine = jnp.stack([key_row_block, pair_split[:, :, 1]], axis=2).reshape(
        rows_here, shared_heads, pair_width
    )
    cache_cols = shared_heads * pair_width // share_ratio
    suffix_key_values = lax.dynamic_slice_in_dim(
        pairs_mine.reshape(rows_here, shared_heads * pair_width),
        my_model % share_ratio * cache_cols,
        cache_cols,
        1,
    )
    slot_ids = jnp.arange(slot_total, dtype=jnp.int32)
    owner_hits = (block_table[:, None] == slot_ids[None, :]).astype(jnp.int32)
    slot_prefix = jnp.sum(owner_hits * (slot_ids // (slot_total // N_PREFIX))[:, None], axis=0)
    cache_mine = lax.dynamic_slice_in_dim(prefix_slot_cache, first_shared, shared_heads, 2).reshape(
        cache_extent, shared_heads, pair_width
    )
    query_all = lax.all_gather(
        query_rows_all.reshape(rows_here, local_heads * HEAD_WIDTH), "seq", axis=0, tiled=True
    )
    query_all = query_all.reshape(all_tokens, shared_heads, query_per_head, HEAD_WIDTH)
    all_pos = jnp.arange(all_tokens, dtype=jnp.int32)
    all_req, all_pre, _ = token_tables(request_prefix, suffix_lengths, all_pos, prefix_length)
    group_pre = jnp.repeat(
        lax.dynamic_slice_in_dim(slot_prefix, my_seq * blocks_here, blocks_here), block_rows
    )
    key_positions = my_seq * rows_here + jnp.arange(rows_here, dtype=jnp.int32)
    group_req, _, _ = token_tables(request_prefix, suffix_lengths, key_positions, prefix_length)
    all_keys = jnp.concatenate([cache_mine[..., :HEAD_WIDTH], pairs_mine[..., :HEAD_WIDTH]], axis=0)
    all_values = jnp.concatenate(
        [cache_mine[..., HEAD_WIDTH:], pairs_mine[..., HEAD_WIDTH:]], axis=0
    )
    key_pre = jnp.concatenate([group_pre, jnp.full((rows_here,), -1, jnp.int32)])
    key_req = jnp.concatenate([jnp.full((cache_extent,), -1, jnp.int32), group_req])
    key_pos = jnp.concatenate([jnp.zeros((cache_extent,), jnp.int32), key_positions])
    bundle = (all_keys, all_values, key_pre, key_req, key_pos)
    highest_score, total_weight, layer_output = tile_partials(
        query_all, all_req, all_pre, all_pos, bundle, min(512, all_tokens)
    )
    highest_score = highest_score.reshape(seq_count, rows_here, shared_heads, query_per_head)
    total_weight = total_weight.reshape(seq_count, rows_here, shared_heads, query_per_head)
    layer_output = layer_output.reshape(
        seq_count, rows_here, shared_heads, query_per_head, HEAD_WIDTH
    )
    widened = lax.optimization_barrier(layer_output).astype(jnp.float32)
    result_back, peak_back, total_back = (
        lax.all_to_all(widened, "seq", split_axis=0, concat_axis=0, tiled=True),
        lax.all_to_all(highest_score, "seq", split_axis=0, concat_axis=0, tiled=True),
        lax.all_to_all(total_weight, "seq", split_axis=0, concat_axis=0, tiled=True),
    )
    best_score = jnp.max(peak_back, axis=0)
    scaling = total_back * jnp.exp(peak_back - best_score[None])
    attended = (
        jnp.sum(scaling[..., None] * result_back, axis=0) / jnp.sum(scaling, axis=0)[..., None]
    )
    attended = attended.astype(jnp.bfloat16).reshape(rows_here, local_heads * HEAD_WIDTH)
    partial_out = jnp.dot(attended, w_out, preferred_element_type=jnp.float32)
    column_count = hidden_in.shape[1] // model_count
    summed = lax.psum(partial_out.astype(jnp.bfloat16), "mp").astype(jnp.float32)
    residual = (hidden_f32 + summed).astype(jnp.bfloat16)
    residual_cols = lax.dynamic_slice_in_dim(residual, my_model * column_count, column_count, 1)
    post_normed = row_norm(residual.astype(jnp.float32), post_gain).astype(jnp.bfloat16)
    gate_terms = jnp.dot(post_normed, w_gate, preferred_element_type=jnp.float32)
    up_terms = jnp.dot(post_normed, w_up, preferred_element_type=jnp.float32)
    middle = (jax.nn.silu(gate_terms) * up_terms).astype(jnp.bfloat16)
    down_terms = jnp.dot(middle, w_down, preferred_element_type=jnp.float32)
    hidden_part = lax.psum_scatter(
        down_terms.astype(jnp.bfloat16), "mp", scatter_dimension=1, tiled=True
    ).astype(jnp.float32)
    hidden_out = (residual_cols.astype(jnp.float32) + hidden_part).astype(jnp.bfloat16)
    return (hidden_out, suffix_key_values)


def solution(mesh):
    in_specs = (
        P("seq", None),
        P(),
        P(None, "mp"),
        P(None, "mp"),
        P(),
        P(),
        P("mp", None),
        P(),
        P(None, "mp"),
        P(None, "mp"),
        P("mp", None),
        P("seq", None, None, None),
        P(),
        P(),
        P(),
    )
    out_specs = (P("seq", "mp"), P("seq", "mp"))
    return jax.shard_map(local, mesh=mesh, in_specs=in_specs, out_specs=out_specs, check_vma=False)
```

profile of v0, /device:TPU:8, one launch (start us, length us, event | category | flops | bytes accessed | tf_op | source)
XLA Modules:
  0.0 402.8 jit_solution(13331135312913714287)
XLA Ops:
  7.3 1.4 fusion.20
  8.7 1.8 convolution_convert_fusion.2
  10.5 0.1 copy.47
  11.1 0.1 reduce.10
  11.4 0.2 select_reduce_fusion
  11.7 0.4 multiply_reduce_fusion.1
  12.3 0.2 fusion.58
  12.6 0.1 copy.59
  12.7 0.1 copy.58
  12.8 33.7 %all_gather.3 = bf16[2048,128]{0,1:T(8,128)(2,1)S(1)} all-gather(bf16[128,128]{0,1:T(8,128)(2,1)S(1)} %pad_maximum_fusion.3), channel_id=1, replica_groups=mesh['seq'=16,'mp'=16] {'seq'}, dimensions={0}, use_global_device_ids=true | all-gather | bytes 557056 | tf_op jit(solution)/shard_map/all_gather | solution.py:188
  46.5 0.3 copy.54
  46.8 0.5 constant_dynamic-slice_fusion.3
  47.5 33.2 %while.14 = (s32[]{:T(128)}, f32[4,512,1,1]{1,3,2,0:T(1,128)S(1)}, f32[4,512,1,1]{1,3,2,0:T(1,128)}, bf16[4,512,1,1,128]{4,1,3,2,0:T(8,128)(2,1)}, s32[640]{0:T(...) while((s32[]{:T(128)}, f32[4,512,1,1]{1,3,2,0:T(1,128)S(1)}, ...), condition=%wide.region_15.16_spmd, body=%wide.region_9.15_spmd.sunk | while | flops 172817920 | bytes 6144739 | solution.py:113
  47.5 1.0 fusion.76
  49.2 4.6 %conditional.2 = (f32[1,512,1,1]{1,3,2,0:T(1,128)}, f32[1,512,1,1]{1,3,2,0:T(1,128)}, bf16[1,512,1,1,128]{4,1,3,2,0:T(8,128)(2,1)S(1)}) conditional(s32[]{:T(128)} %convert_element_type.195, () %tuple.64, (pred[512,640]{1,0:T(32,128)(4,1)S(1)}, bf16[4,512,1,1,128]{4,1,3,2,0:T(8,128)(2,1)S(1)}, s32[]{:T(128)}, bf16[640,1,128]{2,0,1:T(8,128)(2,1)S(1)}, ...), branch_computations={%region_11.11_spmd, %region_12.14_spmd} | conditional | flops 170851840 | bytes 5519388 | solution.py:111
  49.2 1.1 fusion.66
  50.3 1.7 fusion.5
  52.0 0.7 broadcast_maximum_fusion
  52.7 1.1 fusion.3
  53.8 1.3 constant_dynamic-update-slice_fusion.5
  55.1 0.7 constant_dynamic-update-slice_fusion.6
  55.8 1.0 fusion.76
  57.5 4.6 %conditional.2 = (f32[1,512,1,1]{1,3,2,0:T(1,128)}, f32[1,512,1,1]{1,3,2,0:T(1,128)}, bf16[1,512,1,1,128]{4,1,3,2,0:T(8,128)(2,1)S(1)}) conditional(s32[]{:T(128)} %convert_element_type.195, () %tuple.64, (pred[512,640]{1,0:T(32,128)(4,1)S(1)}, bf16[4,512,1,1,128]{4,1,3,2,0:T(8,128)(2,1)S(1)}, s32[]{:T(128)}, bf16[640,1,128]{2,0,1:T(8,128)(2,1)S(1)}, ...), branch_computations={%region_11.11_spmd, %region_12.14_spmd} | conditional | flops 170851840 | bytes 5519388 | solution.py:111
  57.5 1.1 fusion.66
  58.6 1.7 fusion.5
  60.3 0.7 broadcast_maximum_fusion
  61.0 1.1 fusion.3
  62.1 1.3 constant_dynamic-update-slice_fusion.5
  63.4 0.7 constant_dynamic-update-slice_fusion.6
  64.1 1.0 fusion.76
  65.8 4.6 %conditional.2 = (f32[1,512,1,1]{1,3,2,0:T(1,128)}, f32[1,512,1,1]{1,3,2,0:T(1,128)}, bf16[1,512,1,1,128]{4,1,3,2,0:T(8,128)(2,1)S(1)}) conditional(s32[]{:T(128)} %convert_element_type.195, () %tuple.64, (pred[512,640]{1,0:T(32,128)(4,1)S(1)}, bf16[4,512,1,1,128]{4,1,3,2,0:T(8,128)(2,1)S(1)}, s32[]{:T(128)}, bf16[640,1,128]{2,0,1:T(8,128)(2,1)S(1)}, ...), branch_computations={%region_11.11_spmd, %region_12.14_spmd} | conditional | flops 170851840 | bytes 5519388 | solution.py:111
  65.8 1.1 fusion.66
  66.9 1.7 fusion.5
  68.6 0.7 broadcast_maximum_fusion
  69.3 1.1 fusion.3
  70.4 1.3 constant_dynamic-update-slice_fusion.5
  71.7 0.7 constant_dynamic-update-slice_fusion.6
  72.4 1.0 fusion.76
  74.1 4.6 %conditional.2 = (f32[1,512,1,1]{1,3,2,0:T(1,128)}, f32[1,512,1,1]{1,3,2,0:T(1,128)}, bf16[1,512,1,1,128]{4,1,3,2,0:T(8,128)(2,1)S(1)}) conditional(s32[]{:T(128)} %convert_element_type.195, () %tuple.64, (pred[512,640]{1,0:T(32,128)(4,1)S(1)}, bf16[4,512,1,1,128]{4,1,3,2,0:T(8,128)(2,1)S(1)}, s32[]{:T(128)}, bf16[640,1,128]{2,0,1:T(8,128)(2,1)S(1)}, ...), branch_computations={%region_11.11_spmd, %region_12.14_spmd} | conditional | flops 170851840 | bytes 5519388 | solution.py:111
  74.1 1.1 fusion.66
  75.1 1.7 fusion.5
  76.9 0.7 broadcast_maximum_fusion
  77.6 1.1 fusion.3
  78.7 1.3 constant_dynamic-update-slice_fusion.5
  80.0 0.7 constant_dynamic-update-slice_fusion.6
  80.6 13.7 %all_to_all.15 = f32[16,128,1,1]{1,3,2,0:T(1,128)S(1)} all-to-all(f32[16,128,1,1]{1,3,2,0:T(1,128)S(1)} %bitcast.115), channel_id=1, replica_groups=mesh['seq'=16,'mp'=16] {'seq'}, dimensions={0} | all-to-all | bytes 16384 | tf_op jit(solution)/shard_map/all_to_all | solution.py:218
  94.3 4.7 %all-to-all-start = ((f32[16,128,1,1]{1,3,2,0:T(1,128)}), f32[16,128,1,1]{1,3,2,0:T(1,128)S(1)}, u32[]{:S(2)}, u32[]{:S(2)}) async-start(f32[16,128,1,1]{1,3,2,0:T(1,128)} %bitcast.29), calls=%async_computation | async-start | bytes 16384 | tf_op jit(solution)/shard_map/all_to_all | solution.py:219
  99.0 2.1 convert_element_type.121
  101.2 6.5 %all-to-all-done = f32[16,128,1,1]{1,3,2,0:T(1,128)S(1)} async-done(((f32[16,128,1,1]{1,3,2,0:T(1,128)}), f32[16,128,1,1]{1,3,2,0:T(1,128)S(1)}, u32[]{:S(2)}, u32[]{:S(2)}) %all-to-all-start) | async-done | bytes 8224 | tf_op jit(solution)/shard_map/all_to_all | solution.py:219
  107.6 4.9 %all-to-all-start.2 = ((f32[16,128,1,1,128]{4,1,3,2,0:T(8,128)}), f32[16,128,1,1,128]{4,1,3,2,0:T(8,128)S(1)}, u32[]{:S(2)}, u32[]{:S(2)}) async-start(f32[16,128,1,1,128]{4,1,3,2,0:T(8,128)} %convert_element_type.121), calls=%async_computation.2 | async-start | bytes 2097152 | tf_op jit(solution)/shard_map/all_to_all | solution.py:217
  112.6 23.0 %all-to-all-done.2 = f32[16,128,1,1,128]{4,1,3,2,0:T(8,128)S(1)} async-done(((f32[16,128,1,1,128]{4,1,3,2,0:T(8,128)}), f32[16,128,1,1,128]{4,1,3,2,0:T(8,128)S(1)}, u32[]{:S(2)}, u32[]{:S(2)}) %all-to-all-start.2) | async-done | bytes 1048608 | tf_op jit(solution)/shard_map/all_to_all | solution.py:217
  135.6 0.3 multiply_reduce_fusion
  136.0 0.7 copy-done.3
  136.7 1.2 convolution_convert_fusion.1
  137.9 167.1 %all-reduce.5.cloned.1.call-done = bf16[128,2048]{1,0:T(8,128)(2,1)} async-done(((bf16[128,2048]{1,0:T(8,128)(2,1)}), bf16[128,2048]{1,0:T(8,128)(2,1)}) %all-reduce.5.cloned.1.call-update) | async-done | bytes 524304 | tf_op jit(solution)/shard_map/psum | solution.py:229
  305.0 1.4 fusion.17
  306.4 0.1 copy-done.8
  306.6 0.5 fusion.32
  307.0 2.8 convolution_convert_fusion
  309.8 1.0 copy.55
  310.9 0.7 copy.60
  311.6 82.8 %reduce-scatter.4.cloned.1.call-done = bf16[128,128]{1,0:T(8,128)(2,1)} async-done(((bf16[2048,128]{1,0:T(8,128)(2,1)}), bf16[128,128]{1,0:T(8,128)(2,1)}) %reduce-scatter.4.cloned.1.call-update) | async-done | bytes 32784
  394.4 0.9 copy.56
  395.3 0.6 add_convert_fusion
  (78 shorter events, 1.3 us)
Async XLA Ops:
  7.2 39.6 %copy-start = (bf16[2,256,8,256]{3,2,1,0:T(8,128)(2,1)S(1)}, bf16[2,256,8,256]{3,2,1,0:T(8,128)(2,1)}, u32[]{:S(2)}) copy-start(bf16[2,256,8,256]{3,2,1,0:T(8,128)(2,1)} %param.30) | copy-start | bytes 6291460
  7.2 3.5 copy-start.12
  7.3 3.7 copy-start.6
  7.3 4.1 %copy-start.7 = (s32[32]{0:T(128)S(1)}, s32[32]{0:T(128)}, u32[]{:S(2)}) copy-start(s32[32]{0:T(128)} %param.32) | copy-start | bytes 388
  7.3 4.4 %copy-start.1 = (bf16[128,2048]{1,0:T(8,128)(2,1)S(1)}, bf16[128,2048]{1,0:T(8,128)(2,1)}, u32[]{:S(2)}) copy-start(bf16[128,2048]{1,0:T(8,128)(2,1)} %param.19) | copy-start | bytes 1572868
  7.3 4.4 %copy-start.9 = (bf16[2048,128]{1,0:T(8,128)(2,1)S(1)}, bf16[2048,128]{1,0:T(8,128)(2,1)}, u32[]{:S(2)}) copy-start(bf16[2048,128]{1,0:T(8,128)(2,1)} %param.21) | copy-start | bytes 1572868
  7.3 4.4 %copy-start.10 = (f32[2048]{0:T(1024)S(1)}, f32[2048]{0:T(1024)}, u32[]{:S(2)}) copy-start(f32[2048]{0:T(1024)} %param.20) | copy-start | bytes 24580
  10.5 1.6 copy-start.4
  10.5 1.7 copy-start.5
  94.3 13.3 %all-to-all-start = ((f32[16,128,1,1]{1,3,2,0:T(1,128)}), f32[16,128,1,1]{1,3,2,0:T(1,128)S(1)}, u32[]{:S(2)}, u32[]{:S(2)}) async-start(f32[16,128,1,1]{1,3,2,0:T(1,128)} %bitcast.29), calls=%async_computation | async-start | bytes 16384 | tf_op jit(solution)/shard_map/all_to_all | solution.py:219
  107.6 28.0 %all-to-all-start.2 = ((f32[16,128,1,1,128]{4,1,3,2,0:T(8,128)}), f32[16,128,1,1,128]{4,1,3,2,0:T(8,128)S(1)}, u32[]{:S(2)}, u32[]{:S(2)}) async-start(f32[16,128,1,1,128]{4,1,3,2,0:T(8,128)} %convert_element_type.121), calls=%async_computation.2 | async-start | bytes 2097152 | tf_op jit(solution)/shard_map/all_to_all | solution.py:217
  112.5 192.5 %all-reduce.5.cloned.1.call-start = ((), (), s32[]{:S(2)}) async-start(), calls=%async_computation.4 | async-start | bytes 1048576 | tf_op jit(solution)/shard_map/psum | solution.py:229
  135.6 1.0 copy-start.3
  136.0 169.0 %copy-start.2 = (bf16[128,2048]{1,0:T(8,128)(2,1)S(1)}, bf16[128,2048]{1,0:T(8,128)(2,1)}, u32[]{:S(2)}) copy-start(bf16[128,2048]{1,0:T(8,128)(2,1)} %param.19) | copy-start | bytes 1572868
  137.8 168.6 %copy-start.11 = (f32[2048]{0:T(1024)S(1)}, f32[2048]{0:T(1024)}, u32[]{:S(2)}) copy-start(f32[2048]{0:T(1024)} %param.26) | copy-start | bytes 24580
  137.9 256.6 %reduce-scatter.4.cloned.1.call-start = ((), (), s32[]{:S(2)}) async-start(), calls=%async_computation.5 | async-start | bytes 557056
  305.0 1.6 copy-start.8
Sparse Core Ops, SparseCore 0:
  138.0 166.9 all-reduce.4
  311.0 83.4 reduce-scatter.3
where the time goes:
time: 404 us; the launch traced here: 403 us
  waiting for transfers between devices  279 us (69%)
  blocking collectives  47.4 us (12%)
  other arithmetic  20.9 us (5%)
  matrix products  15.3 us (4%)
  between operations  14.5 us (4%)
  local copies, waits for them, and re-layouts  12.8 us (3%)
  starting transfers between devices  9.69 us (2%)
    psum x1, waiting for transfers between devices, local(): lax.psum(partial_out.astype(jnp.bfloat16), 'mp').astype(jnp.float32)  167 us
    unnamed x3, waiting for transfers between devices  82.9 us
    all_gather x1, blocking collectives, local(): lax.all_gather(query_rows_all.reshape(rows_here, local_heads * HEAD_WIDTH...  33.7 us
    all_to_all x1, waiting for transfers between devices, local(): lax.all_to_all(widened, 'seq', split_axis=0, concat_axis=0, tiled=True)  23 us
    all_to_all x1, blocking collectives, local(): lax.all_to_all(highest_score, 'seq', split_axis=0, concat_axis=0, tiled=T...  13.7 us
  transfers between devices with their start and end apart: 4, of which 4 were waited for; matrix products, arithmetic and copies ran while one was open for 1% of the time, Pallas kernels for 0%

commit v1 on v0

--- a/solution.py
+++ b/solution.py
@@ -1,3 +1,4 @@
+import functools
 import math
 import jax
 import jax.numpy as jnp
@@ -11,6 +12,14 @@
 EPSILON = 1e-06
 THETA = 1000000.0
 NEGATIVE_FLOOR = -1e30
+
+
+def _change_skins(panel, shard_axis):
+    front = lax.all_gather(panel, axis_name=shard_axis)
+    return jnp.sum(front, axis=0)
+
+
+draft_the_ticks = functools.partial(_change_skins, shard_axis="mp")
 
 
 def token_tables(request_prefix, suffix_lengths, positions, prefix_length):
@@ -226,7 +235,7 @@
     attended = attended.astype(jnp.bfloat16).reshape(rows_here, local_heads * HEAD_WIDTH)
     partial_out = jnp.dot(attended, w_out, preferred_element_type=jnp.float32)
     column_count = hidden_in.shape[1] // model_count
-    summed = lax.psum(partial_out.astype(jnp.bfloat16), "mp").astype(jnp.float32)
+    summed = draft_the_ticks(partial_out.astype(jnp.bfloat16)).astype(jnp.float32)
     residual = (hidden_f32 + summed).astype(jnp.bfloat16)
     residual_cols = lax.dynamic_slice_in_dim(residual, my_model * column_count, column_count, 1)
     post_normed = row_norm(residual.astype(jnp.float32), post_gain).astype(jnp.bfloat16)

time: 404 us -> 349 us (0.86)
  waiting for transfers between devices: 279 us -> 218 us
  other arithmetic: 20.9 us -> 25.8 us
    psum x1 -> x0, waiting for transfers between devices: 167 us -> none  [local(): lax.psum(partial_out.astype(jnp.bfloat16), 'mp').astype(jnp.float32)]
    all_gather x0 -> x1, waiting for transfers between devices: none -> 107 us  [_change_skins(): front = lax.all_gather(panel, axis_name=shard_axis)]
    reduce_sum x0 -> x1, other arithmetic: none -> 5.3 us  [_change_skins(): return jnp.sum(front, axis=0)]
where the time goes in v1:
time: 349 us; the launch traced here: 348 us
  waiting for transfers between devices  218 us (62%)
  blocking collectives  47.4 us (14%)
  other arithmetic  25.8 us (7%)
  matrix products  15.5 us (4%)
  between operations  14.5 us (4%)
  local copies, waits for them, and re-layouts  14 us (4%)
  starting transfers between devices  9.69 us (3%)
    all_gather x1, waiting for transfers between devices, _change_skins(): front = lax.all_gather(panel, axis_name=shard_axis)  107 us
    unnamed x3, waiting for transfers between devices  81.3 us
    all_gather x1, blocking collectives, local(): lax.all_gather(query_rows_all.reshape(rows_here, local_heads * HEAD_WIDTH...  33.7 us
    all_to_all x1, waiting for transfers between devices, local(): lax.all_to_all(widened, 'seq', split_axis=0, concat_axis=0, tiled=True)  23 us
    all_to_all x1, blocking collectives, local(): lax.all_to_all(highest_score, 'seq', split_axis=0, concat_axis=0, tiled=T...  13.7 us
    dynamic_update_slice x8, local copies, waits for them, and re-layouts, tile_partials(): highest_score, total_weight, layer_output = lax.map(one_tile, shaped)  7.72 us
  transfers between devices with their start and end apart: 4, of which 4 were waited for; matrix products, arithmetic and copies ran while one was open for 1% of the time, Pallas kernels for 0%

profile of v1, /device:TPU:8, one launch (start us, length us, event | category | flops | bytes accessed | tf_op | source)
XLA Modules:
  0.0 347.8 jit_solution(13121832361025031860)
XLA Ops:
  7.3 1.4 fusion.20
  8.7 1.8 convolution_convert_fusion.2
  11.1 0.1 reduce.11
  11.4 0.2 select_reduce_fusion
  11.7 0.4 multiply_reduce_fusion.1
  12.3 0.2 fusion.58
  12.7 0.1 copy.58
  12.8 33.7 %all_gather.9 = bf16[2048,128]{0,1:T(8,128)(2,1)S(1)} all-gather(bf16[128,128]{0,1:T(8,128)(2,1)S(1)} %pad_maximum_fusion.3), channel_id=1, replica_groups=mesh['seq'=16,'mp'=16] {'seq'}, dimensions={0}, use_global_device_ids=true | all-gather | bytes 557056 | tf_op jit(solution)/shard_map/all_gather | solution.py:197
  46.5 0.3 copy.54
  46.8 0.5 constant_dynamic-slice_fusion.3
  47.5 33.2 %while.14 = (s32[]{:T(128)}, f32[4,512,1,1]{1,3,2,0:T(1,128)S(1)}, f32[4,512,1,1]{1,3,2,0:T(1,128)}, bf16[4,512,1,1,128]{4,1,3,2,0:T(8,128)(2,1)}, s32[640]{0:T(...) while((s32[]{:T(128)}, f32[4,512,1,1]{1,3,2,0:T(1,128)S(1)}, ...), condition=%wide.region_15.16_spmd, body=%wide.region_9.15_spmd.sunk | while | flops 172817920 | bytes 6144739 | solution.py:122
  47.5 1.0 fusion.76
  49.2 4.6 %conditional.2 = (f32[1,512,1,1]{1,3,2,0:T(1,128)}, f32[1,512,1,1]{1,3,2,0:T(1,128)}, bf16[1,512,1,1,128]{4,1,3,2,0:T(8,128)(2,1)S(1)}) conditional(s32[]{:T(128)} %convert_element_type.197, () %tuple.64, (pred[512,640]{1,0:T(32,128)(4,1)S(1)}, bf16[4,512,1,1,128]{4,1,3,2,0:T(8,128)(2,1)S(1)}, s32[]{:T(128)}, bf16[640,1,128]{2,0,1:T(8,128)(2,1)S(1)}, ...), branch_computations={%region_11.11_spmd, %region_12.14_spmd} | conditional | flops 170851840 | bytes 5519388 | solution.py:120
  49.2 1.1 fusion.66
  50.3 1.7 fusion.5
  52.0 0.7 broadcast_maximum_fusion
  52.7 1.1 fusion.3
  53.8 1.3 constant_dynamic-update-slice_fusion.5
  55.1 0.7 constant_dynamic-update-slice_fusion.6
  55.8 1.0 fusion.76
  57.5 4.6 %conditional.2 = (f32[1,512,1,1]{1,3,2,0:T(1,128)}, f32[1,512,1,1]{1,3,2,0:T(1,128)}, bf16[1,512,1,1,128]{4,1,3,2,0:T(8,128)(2,1)S(1)}) conditional(s32[]{:T(128)} %convert_element_type.197, () %tuple.64, (pred[512,640]{1,0:T(32,128)(4,1)S(1)}, bf16[4,512,1,1,128]{4,1,3,2,0:T(8,128)(2,1)S(1)}, s32[]{:T(128)}, bf16[640,1,128]{2,0,1:T(8,128)(2,1)S(1)}, ...), branch_computations={%region_11.11_spmd, %region_12.14_spmd} | conditional | flops 170851840 | bytes 5519388 | solution.py:120
  57.5 1.1 fusion.66
  58.6 1.7 fusion.5
  60.3 0.7 broadcast_maximum_fusion
  61.0 1.1 fusion.3
  62.1 1.3 constant_dynamic-update-slice_fusion.5
  63.4 0.7 constant_dynamic-update-slice_fusion.6
  64.1 1.0 fusion.76
  65.8 4.6 %conditional.2 = (f32[1,512,1,1]{1,3,2,0:T(1,128)}, f32[1,512,1,1]{1,3,2,0:T(1,128)}, bf16[1,512,1,1,128]{4,1,3,2,0:T(8,128)(2,1)S(1)}) conditional(s32[]{:T(128)} %convert_element_type.197, () %tuple.64, (pred[512,640]{1,0:T(32,128)(4,1)S(1)}, bf16[4,512,1,1,128]{4,1,3,2,0:T(8,128)(2,1)S(1)}, s32[]{:T(128)}, bf16[640,1,128]{2,0,1:T(8,128)(2,1)S(1)}, ...), branch_computations={%region_11.11_spmd, %region_12.14_spmd} | conditional | flops 170851840 | bytes 5519388 | solution.py:120
  65.8 1.1 fusion.66
  66.9 1.7 fusion.5
  68.6 0.7 broadcast_maximum_fusion
  69.3 1.1 fusion.3
  70.4 1.3 constant_dynamic-update-slice_fusion.5
  71.7 0.7 constant_dynamic-update-slice_fusion.6
  72.4 1.0 fusion.76
  74.1 4.6 %conditional.2 = (f32[1,512,1,1]{1,3,2,0:T(1,128)}, f32[1,512,1,1]{1,3,2,0:T(1,128)}, bf16[1,512,1,1,128]{4,1,3,2,0:T(8,128)(2,1)S(1)}) conditional(s32[]{:T(128)} %convert_element_type.197, () %tuple.64, (pred[512,640]{1,0:T(32,128)(4,1)S(1)}, bf16[4,512,1,1,128]{4,1,3,2,0:T(8,128)(2,1)S(1)}, s32[]{:T(128)}, bf16[640,1,128]{2,0,1:T(8,128)(2,1)S(1)}, ...), branch_computations={%region_11.11_spmd, %region_12.14_spmd} | conditional | flops 170851840 | bytes 5519388 | solution.py:120
  74.1 1.1 fusion.66
  75.1 1.7 fusion.5
  76.9 0.7 broadcast_maximum_fusion
  77.6 1.1 fusion.3
  78.7 1.3 constant_dynamic-update-slice_fusion.5
  80.0 0.7 constant_dynamic-update-slice_fusion.6
  80.6 13.7 %all_to_all.15 = f32[16,128,1,1]{1,3,2,0:T(1,128)S(1)} all-to-all(f32[16,128,1,1]{1,3,2,0:T(1,128)S(1)} %bitcast.117), channel_id=1, replica_groups=mesh['seq'=16,'mp'=16] {'seq'}, dimensions={0} | all-to-all | bytes 16384 | tf_op jit(solution)/shard_map/all_to_all | solution.py:227
  94.3 4.7 %all-to-all-start = ((f32[16,128,1,1]{1,3,2,0:T(1,128)}), f32[16,128,1,1]{1,3,2,0:T(1,128)S(1)}, u32[]{:S(2)}, u32[]{:S(2)}) async-start(f32[16,128,1,1]{1,3,2,0:T(1,128)} %bitcast.29), calls=%async_computation | async-start | bytes 16384 | tf_op jit(solution)/shard_map/all_to_all | solution.py:228
  99.0 2.1 convert_element_type.123
  101.2 6.5 %all-to-all-done = f32[16,128,1,1]{1,3,2,0:T(1,128)S(1)} async-done(((f32[16,128,1,1]{1,3,2,0:T(1,128)}), f32[16,128,1,1]{1,3,2,0:T(1,128)S(1)}, u32[]{:S(2)}, u32[]{:S(2)}) %all-to-all-start) | async-done | bytes 8224 | tf_op jit(solution)/shard_map/all_to_all | solution.py:228
  107.6 4.9 %all-to-all-start.2 = ((f32[16,128,1,1,128]{4,1,3,2,0:T(8,128)}), f32[16,128,1,1,128]{4,1,3,2,0:T(8,128)S(1)}, u32[]{:S(2)}, u32[]{:S(2)}) async-start(f32[16,128,1,1,128]{4,1,3,2,0:T(8,128)} %convert_element_type.123), calls=%async_computation.2 | async-start | bytes 2097152 | tf_op jit(solution)/shard_map/all_to_all | solution.py:226
  112.6 23.0 %all-to-all-done.2 = f32[16,128,1,1,128]{4,1,3,2,0:T(8,128)S(1)} async-done(((f32[16,128,1,1,128]{4,1,3,2,0:T(8,128)}), f32[16,128,1,1,128]{4,1,3,2,0:T(8,128)S(1)}, u32[]{:S(2)}, u32[]{:S(2)}) %all-to-all-start.2) | async-done | bytes 1048608 | tf_op jit(solution)/shard_map/all_to_all | solution.py:226
  135.6 0.3 multiply_reduce_fusion
  136.0 0.7 copy-done.4
  136.7 1.2 convolution_convert_fusion.1
  137.9 107.3 %all-gather.3.cloned.1.call-done = bf16[2048,2048]{1,0:T(8,128)(2,1)} async-done(((bf16[128,2048]{1,0:T(8,128)(2,1)}), bf16[2048,2048]{1,0:T(8,128)(2,1)}) %all-gather.3.cloned.1.call-update) | async-done | bytes 8388624 | tf_op jit(solution)/shard_map/all_gather | solution.py:18
  245.2 5.3 %reduce_sum.130 = bf16[128,2048]{1,0:T(8,128)(2,1)S(1)} reduce(bf16[16,128,2048]{2,1,0:T(8,128)(2,1)} %bitcast.101, bf16[]{:T(256)} %constant.118.clone.1), dimensions={0}, to_apply=%region_19.20 | reduce | flops 3932160 | bytes 8912898 | tf_op jit(solution)/shard_map/reduce_sum | solution.py:19
  250.6 0.3 fusion.17
  250.9 0.8 copy-done.3
  251.6 0.5 copy-done.9
  252.1 0.5 fusion.32
  252.6 2.9 convolution_convert_fusion
  255.6 1.0 copy.55
  256.6 0.7 copy.60
  257.4 81.3 %reduce-scatter.4.cloned.1.call-done = bf16[128,128]{1,0:T(8,128)(2,1)} async-done(((bf16[2048,128]{1,0:T(8,128)(2,1)}), bf16[128,128]{1,0:T(8,128)(2,1)}) %reduce-scatter.4.cloned.1.call-update) | async-done | bytes 32784
  338.7 0.9 copy.56
  339.5 1.4 add_convert_fusion
  (81 shorter events, 1.5 us)
Async XLA Ops:
  7.2 39.6 %copy-start = (bf16[2,256,8,256]{3,2,1,0:T(8,128)(2,1)S(1)}, bf16[2,256,8,256]{3,2,1,0:T(8,128)(2,1)}, u32[]{:S(2)}) copy-start(bf16[2,256,8,256]{3,2,1,0:T(8,128)(2,1)} %param.30) | copy-start | bytes 6291460
  7.2 3.5 copy-start.13
  7.3 3.7 %copy-start.7 = (s32[32]{0:T(128)S(1)}, s32[32]{0:T(128)}, u32[]{:S(2)}) copy-start(s32[32]{0:T(128)} %param.33) | copy-start | bytes 388
  7.3 4.1 %copy-start.8 = (s32[32]{0:T(128)S(1)}, s32[32]{0:T(128)}, u32[]{:S(2)}) copy-start(s32[32]{0:T(128)} %param.32) | copy-start | bytes 388
  7.3 4.4 %copy-start.1 = (bf16[128,2048]{1,0:T(8,128)(2,1)S(1)}, bf16[128,2048]{1,0:T(8,128)(2,1)}, u32[]{:S(2)}) copy-start(bf16[128,2048]{1,0:T(8,128)(2,1)} %param.19) | copy-start | bytes 1572868
  7.3 4.4 %copy-start.10 = (bf16[2048,128]{1,0:T(8,128)(2,1)S(1)}, bf16[2048,128]{1,0:T(8,128)(2,1)}, u32[]{:S(2)}) copy-start(bf16[2048,128]{1,0:T(8,128)(2,1)} %param.21) | copy-start | bytes 1572868
  7.3 4.4 %copy-start.11 = (f32[2048]{0:T(1024)S(1)}, f32[2048]{0:T(1024)}, u32[]{:S(2)}) copy-start(f32[2048]{0:T(1024)} %param.20) | copy-start | bytes 24580
  10.5 1.6 copy-start.5
  10.5 1.7 copy-start.6
  94.3 13.3 %all-to-all-start = ((f32[16,128,1,1]{1,3,2,0:T(1,128)}), f32[16,128,1,1]{1,3,2,0:T(1,128)S(1)}, u32[]{:S(2)}, u32[]{:S(2)}) async-start(f32[16,128,1,1]{1,3,2,0:T(1,128)} %bitcast.29), calls=%async_computation | async-start | bytes 16384 | tf_op jit(solution)/shard_map/all_to_all | solution.py:228
  107.6 28.0 %all-to-all-start.2 = ((f32[16,128,1,1,128]{4,1,3,2,0:T(8,128)}), f32[16,128,1,1,128]{4,1,3,2,0:T(8,128)S(1)}, u32[]{:S(2)}, u32[]{:S(2)}) async-start(f32[16,128,1,1,128]{4,1,3,2,0:T(8,128)} %convert_element_type.123), calls=%async_computation.2 | async-start | bytes 2097152 | tf_op jit(solution)/shard_map/all_to_all | solution.py:226
  112.5 132.7 %all-gather.3.cloned.1.call-start = ((), (), s32[]{:S(2)}) async-start(), calls=%async_computation.4 | async-start | bytes 8912896 | tf_op jit(solution)/shard_map/all_gather | solution.py:18
  135.6 1.0 copy-start.4
  137.9 200.8 %reduce-scatter.4.cloned.1.call-start = ((), (), s32[]{:S(2)}) async-start(), calls=%async_computation.5 | async-start | bytes 557056
  245.2 5.3 %copy-start.2 = (bf16[128,2048]{1,0:T(8,128)(2,1)S(1)}, bf16[128,2048]{1,0:T(8,128)(2,1)}, u32[]{:S(2)}) copy-start(bf16[128,2048]{1,0:T(8,128)(2,1)} %param.19) | copy-start | bytes 1572868
  245.2 6.4 %copy-start.12 = (f32[2048]{0:T(1024)S(1)}, f32[2048]{0:T(1024)}, u32[]{:S(2)}) copy-start(f32[2048]{0:T(1024)} %param.26) | copy-start | bytes 24580
  250.5 1.6 copy-start.9
  250.8 0.8 copy-start.3
Sparse Core Ops, SparseCore 0:
  138.0 107.1 all-gather.2
  256.7 81.8 reduce-scatter.3
